TPU v7x, 128 devices: a whole 4x4x4 slice. The times are simulated.
128 devices in a mesh: gx: 4 (over x), gy: 32 (over z, y, core).
Axes of the slice: x: 4, y: 4, z: 4, core: 2. Of those that a mesh axis runs over, the one named last changes fastest.
Arguments:
- gcm_state: float32 [3, 58, 16384], P(None, None, ('gx', 'gy')), may hold values from -4 to 4
- crm_state: float32 [2, 58, 524288], P(None, None, ('gx', 'gy')), may hold values from -4 to 4
- send_source: int32 [16384], P(('gx', 'gy')), may hold values from 0 to 127, as said below
- group_owner: int32 [4096], P(('gx', 'gy')), may hold values from 0 to 31, as said below
Outputs:
- tendency: float32 [2, 58, 16384], P(None, None, ('gx', 'gy'))
- crm_next: float32 [2, 58, 1048576], P(None, None, ('gx', 'gy'))
Inputs may be any that keep to these rules, and one draw needn't show every extreme that they name: `send_source`: each aligned block of 128 entries is a permutation of 0 to 127. `group_owner`: A home device gives at most 2 groups to one owner; in every draw one owner in each gx row receives 2 groups from every home of its row.
All inputs are finite; a program needn't handle non-finite values.
Results may differ from a plain program's by a relative error of at most 0.0001.
Values sent between devices are 32-bit elements; how exact they have to be, the bound alone decides.
A program may use at most 256 MiB of HBM per device.

v0:
```python
import functools

import jax
import jax.numpy as jnp
from jax import lax
from jax.experimental import pallas as pl
from jax.experimental.pallas import tpu as pltpu
from jax.sharding import PartitionSpec as P

CRM_X = 32
LEV = 58
PAD = 64
LANES = 128
NX = 4
NY = 32
GROUPS = 32
F32 = jnp.float32
BF16 = jnp.bfloat16
MESH = pl.DeviceIdType.MESH

NN = (((1,), (0,)), ((), ()))
NT = (((1,), (1,)), ((), ()))

OFFSETS = [(a, b, c) for a in range(4) for b in range(4) for c in range(2) if (a, b, c) != (0, 0, 0)]
ORDER = [29, 12, 4, 23, 17, 8, 26, 1, 14, 20, 6, 30, 10, 3, 25, 16, 22, 9, 0, 27, 13, 18, 5, 24, 11, 2, 28, 19, 7, 15, 21]


def shifted(gy, offset):
    dz, dy, dc = offset
    z, y, c = gy // 8, (gy // 2) % 4, gy % 2
    return (((z + dz) % 4) * 4 + (y + dy) % 4) * 2 + (c + dc) % 2


def split(x, pieces):
    out = []
    for _ in range(pieces - 1):
        hi = x.astype(BF16)
        out.append(hi)
        x = x - hi.astype(F32)
    out.append(x.astype(BF16))
    return out


def dot(a, b, dims):
    return lax.dot_general(a, b, dims, preferred_element_type=F32)


def pick(x, onehot, dims=NN):
    parts = [dot(p, onehot, dims) for p in split(x, 3)]
    return parts[0] + (parts[1] + parts[2])


def pick_rows(onehot, x, dims=NN):
    parts = [dot(onehot, p, dims) for p in split(x, 3)]
    return parts[0] + (parts[1] + parts[2])


def iota(shape, dim):
    return lax.broadcasted_iota(jnp.int32, shape, dim)


def hot(cond):
    return jnp.where(cond, 1.0, 0.0).astype(BF16)


def padded(s):
    if s.shape[0] == PAD:
        return s
    return jnp.concatenate([s, jnp.zeros((PAD - LEV, s.shape[1]), F32)], axis=0)


def step_kernel(
    slot_ref, source_ref, gcm_ref, crm_hbm,
    out_ref, tend_ref,
    crm, gpad, x1s, x1r, x2s, x2r, r1s, r1r, r2s, r2r, spread, spread_of, fin, warm, send, mean_sc, coef,
    crm_sem, own_sem, s1, v1, s2, v2, s3, v3, s4, v4, s5, v5,
):
    gx = lax.axis_index("gx")
    gy = lax.axis_index("gy")
    peers_x = [(gx + d) % NX for d in (1, 2, 3)]
    peers_y = [shifted(gy, OFFSETS[i]) for i in ORDER]

    barrier = pltpu.get_barrier_semaphore()
    for tx in peers_x:
        pl.semaphore_signal(barrier, inc=1, device_id={"gx": tx}, device_id_type=MESH)
    for ty in peers_y:
        pl.semaphore_signal(barrier, inc=1, device_id={"gy": ty}, device_id_type=MESH)

    load = pltpu.make_async_copy(crm_hbm, crm, crm_sem)
    load.start()

    gpad[...] = jnp.zeros((4, PAD, LANES), F32)
    gpad[0:3, 0:LEV, :] = gcm_ref[...]
    source = source_ref[...]
    chosen = hot(iota((LANES, LANES), 0) == source)
    packed = pick(gpad[...].reshape(4 * PAD, LANES), chosen)
    x1s[0] = packed[0:128].T
    x1s[1] = packed[128:256].T

    pl.semaphore_wait(barrier, 3 + 31)

    own_rows = pl.ds(pl.multiple_of(gx * 32, 32), 32)
    stage1 = []
    for i, tx in enumerate(peers_x):
        copy = pltpu.make_async_remote_copy(
            src_ref=x1s.at[:, pl.ds(pl.multiple_of(tx * 32, 32), 32), :],
            dst_ref=x1r.at[:, own_rows, :],
            send_sem=s1.at[i], recv_sem=v1.at[i], device_id={"gx": tx}, device_id_type=MESH,
        )
        copy.start()
        stage1.append(copy)
    x1r[:, own_rows, :] = x1s[:, own_rows, :]

    def fill(g, carry):
        cols = g * 4 + iota((LANES, LANES), 1) // CRM_X
        spread_of[:, pl.ds(pl.multiple_of(g * LANES, LANES), LANES)] = hot(iota((LANES, LANES), 0) == cols)
        return carry
    lax.fori_loop(0, GROUPS, fill, 0)

    for copy in stage1:
        copy.wait()
    row = iota((256, LANES), 0)
    col = iota((256, LANES), 1)
    here = (row // 8 == col % 32)
    perm = [hot(here & (row % 8 == (col // 32) * 2 + h)) for h in range(2)]
    x2s[...] = (pick_rows(perm[0], x1r[0]) + pick_rows(perm[1], x1r[1])).reshape(32, 8, LANES)
    stage2 = []
    for i, ty in enumerate(peers_y):
        copy = pltpu.make_async_remote_copy(
            src_ref=x2s.at[ty], dst_ref=x2r.at[gy],
            send_sem=s2.at[i], recv_sem=v2.at[i], device_id={"gy": ty}, device_id_type=MESH,
        )
        copy.start()
        stage2.append(copy)
    x2r[gy] = x2s[gy]

    load.wait()

    def column_means(ref_a, ref_b, out_ref):
        out_ref[...] = jnp.zeros((2 * PAD, LANES), F32)

        def add(i, carry):
            lanes = pl.ds(pl.multiple_of(i * 512, 512), 512)
            both = jnp.concatenate([padded(ref_a[:, lanes]), padded(ref_b[:, lanes])], axis=0)
            hi, lo = split(both, 2)
            e = spread_of[:, lanes]
            out_ref[...] += dot(hi, e, NT) + dot(lo, e, NT)
            return carry
        lax.fori_loop(0, 8, add, 0)
        return out_ref[...] * (1.0 / CRM_X)

    level = iota((PAD, LANES), 0)
    means = column_means(crm.at[0], crm.at[1], mean_sc)

    def below(s):
        return jnp.where(level == 0, s, pltpu.roll(s, 1, 0))

    def above(s):
        return jnp.where(level == LEV - 1, s, pltpu.roll(s, PAD - 1, 0))

    moved_mean = []
    for f in range(2):
        m = means[f * PAD:(f + 1) * PAD]
        moved_mean.append(0.8 * m + 0.1 * (below(m) + above(m)))

    for copy in stage2:
        copy.wait()
    landed = x2r[...].reshape(256, LANES).T
    first = pick(landed, perm[0])
    wind = pick(landed[0:PAD], perm[1])
    target = [first[0:PAD], first[PAD:128]]
    columns = jnp.concatenate(
        [0.125 * jnp.tanh(wind)] + [0.5 * (target[f] - moved_mean[f]) for f in range(2)], axis=0)
    hi, lo = split(columns, 2)
    coef[0] = hi
    coef[1] = lo

    def spread_out(i, carry):
        lanes = pl.ds(pl.multiple_of(i * 512, 512), 512)
        e = spread_of[:, lanes]
        spread[:, lanes] = dot(coef[0], e, NN) + dot(coef[1], e, NN)
        return carry
    lax.fori_loop(0, 8, spread_out, 0)

    x = iota((PAD, LANES), 1) % CRM_X

    def advance(s, speed, shift):
        west = jnp.where(x == 0, pltpu.roll(s, LANES - 31, 1), pltpu.roll(s, 1, 1))
        east = jnp.where(x == CRM_X - 1, pltpu.roll(s, 31, 1), pltpu.roll(s, LANES - 1, 1))
        return (0.6 * s + 0.1 * ((east + west) + (below(s) + above(s))) - speed * (east - west)) + shift

    def one_group(g, carry):
        lanes = pl.ds(pl.multiple_of(g * LANES, LANES), LANES)
        speed = spread[0:PAD, lanes]
        energy = advance(padded(crm[0, :, lanes]), speed, spread[PAD:2 * PAD, lanes])
        water = advance(padded(crm[1, :, lanes]), speed, spread[2 * PAD:3 * PAD, lanes])
        base = 0.5 * energy + (1.25 * water - 0.625)
        half = base - 0.625 * jnp.tanh(0.5 * energy)
        half = base - 0.625 * jnp.tanh(half)
        half = base - 0.625 * jnp.tanh(half)
        final = 0.8 * water + (0.1 + 0.1 * jnp.tanh(half))
        warm[0, :, lanes] = half + half
        warm[1, :, lanes] = final
        fin[g, 0] = energy[0:LEV]
        fin[g, 1] = final[0:LEV]
        return carry
    lax.fori_loop(0, GROUPS, one_group, 0)

    ends = column_means(warm.at[0], warm.at[1], mean_sc)
    tendency = ends - first
    back = hot((row // 8 == col % 32) & (row % 8 == col // 32))
    r1s[...] = pick_rows(back, tendency, NT).reshape(32, 8, LANES)
    stage3 = []
    for i, ty in enumerate(peers_y):
        copy = pltpu.make_async_remote_copy(
            src_ref=r1s.at[ty], dst_ref=r1r.at[gy],
            send_sem=s3.at[i], recv_sem=v3.at[i], device_id={"gy": ty}, device_id_type=MESH,
        )
        copy.start()
        stage3.append(copy)
    r1r[gy] = r1s[gy]

    def gather(i, d):
        for r in range(2):
            g = slot_ref[d * 2 + r]
            block = fin[jnp.maximum(g, 0)]
            send[i, :, :, r * LANES:(r + 1) * LANES] = jnp.where(g >= 0, block, 0.0)

    own_lanes = pl.ds(pl.multiple_of(gy * 256, 256), 256)
    moves = []
    for i, ty in enumerate(peers_y):
        gather(i, ty)
        copy = pltpu.make_async_remote_copy(
            src_ref=send.at[i], dst_ref=out_ref.at[:, :, own_lanes],
            send_sem=s5.at[i], recv_sem=v5.at[i], device_id={"gy": ty}, device_id_type=MESH,
        )
        copy.start()
        moves.append(copy)
    gather(31, gy)
    own = pltpu.make_async_copy(send.at[31], out_ref.at[:, :, own_lanes], own_sem)
    own.start()

    for copy in stage3:
        copy.wait()
    rows = iota((LANES, 256), 0)
    cols = iota((LANES, 256), 1)
    r2s[...] = pick_rows(hot((rows % 32 == cols // 8) & (rows // 32 == cols % 8)), r1r[...].reshape(256, LANES))
    stage4 = []
    for i, tx in enumerate(peers_x):
        copy = pltpu.make_async_remote_copy(
            src_ref=r2s.at[pl.ds(pl.multiple_of(tx * 32, 32), 32), :], dst_ref=r2r.at[own_rows, :],
            send_sem=s4.at[i], recv_sem=v4.at[i], device_id={"gx": tx}, device_id_type=MESH,
        )
        copy.start()
        stage4.append(copy)
    r2r[own_rows, :] = r2s[own_rows, :]
    for copy in stage4:
        copy.wait()
    placed = pick(r2r[...].T, chosen, NT)
    tend_ref[0] = placed[0:LEV]
    tend_ref[1] = placed[PAD:PAD + LEV]

    own.wait()
    for copy in moves:
        copy.wait()


def slots_of(group_owner):
    g = jnp.arange(GROUPS, dtype=jnp.int32)[None, :]
    same = group_owner[None, :] == jnp.arange(NY, dtype=jnp.int32)[:, None]
    low = jnp.min(jnp.where(same, g, GROUPS), axis=1)
    high = jnp.max(jnp.where(same, g, -1), axis=1)
    return jnp.stack([jnp.where(high < 0, -1, low), jnp.where(high > low, high, -1)], axis=1).reshape(2 * NY)


def on_device(gcm_state, crm_state, send_source, group_owner):
    vm = pltpu.VMEM
    dma = pltpu.SemaphoreType.DMA
    crm_next, tendency = pl.pallas_call(
        step_kernel,
        out_shape=(jax.ShapeDtypeStruct((2, LEV, 8192), F32), jax.ShapeDtypeStruct((2, LEV, LANES), F32)),
        in_specs=[
            pl.BlockSpec(memory_space=pltpu.SMEM),
            pl.BlockSpec(memory_space=pltpu.VMEM),
            pl.BlockSpec(memory_space=pltpu.VMEM),
            pl.BlockSpec(memory_space=pl.ANY),
        ],
        out_specs=(pl.BlockSpec(memory_space=pl.ANY), pl.BlockSpec(memory_space=pltpu.VMEM)),
        scratch_shapes=[
            vm((2, LEV, 4096), F32), vm((4, PAD, LANES), F32),
            vm((2, 128, LANES), F32), vm((2, 128, LANES), F32),
            vm((32, 8, LANES), F32), vm((32, 8, LANES), F32),
            vm((32, 8, LANES), F32), vm((32, 8, LANES), F32),
            vm((128, LANES), F32), vm((128, LANES), F32),
            vm((3 * PAD, 4096), F32), vm((LANES, 4096), BF16),
            vm((GROUPS, 2, LEV, LANES), F32), vm((2, PAD, 4096), F32),
            vm((32, 2, LEV, 256), F32), vm((2 * PAD, LANES), F32), vm((2, 3 * PAD, LANES), BF16),
            dma, dma, dma((3,)), dma((3,)), dma((31,)), dma((31,)), dma((31,)), dma((31,)),
            dma((3,)), dma((3,)), dma((31,)), dma((31,)),
        ],
        compiler_params=pltpu.CompilerParams(collective_id=0, has_side_effects=True, vmem_limit_bytes=48 << 20),
    )(slots_of(group_owner), send_source.reshape(1, LANES), gcm_state, crm_state)
    return tendency, crm_next


def solution(mesh):
    spec = P(None, None, ("gx", "gy"))
    flat = P(("gx", "gy"))
    return jax.shard_map(
        on_device, mesh=mesh, in_specs=(spec, spec, flat, flat), out_specs=(spec, spec), check_vma=False)
```

profile of v0, /device:TPU:1, one launch (start us, length us, event | category | flops | bytes accessed | tf_op | source)
XLA Modules:
  0.0 95.0 jit_solution(3754690372561259108)
XLA Ops:
  0.6 0.0 copy-start.1
  0.6 0.0 copy-start
  0.6 0.8 select_reduce_fusion.1
  1.5 0.1 copy.14
  1.6 0.1 reshape.39.slot_ref
  1.7 2.6 %copy.15.crm_hbm = f32[2,58,4096]{2,1,0:T(8,128)S(1)} copy(f32[2,58,4096]{2,0,1:T(2,128)} %param.5) | data formatting | bytes 3801088 | tf_op args[1]
  4.3 0.0 copy-done.1
  4.3 0.0 copy-done
  4.3 83.0 %shard_map.59 = (f32[2,58,8192]{2,1,0:T(8,128)}, f32[2,58,128]{2,1,0:T(8,128)S(1)}) custom-call(s32[64]{0:T(128)S(1)} %reshape.39.slot_ref, s32[1,128]{1,0:T(1,128)S(1)} %bitcast.7, f32[3,58,128]{2,1,0:T(8,128)S(1)} %copy-done, f32[2,58,4096]{2,1,0:T(8,128)S(1)} %copy.15.crm_hbm), custom_call_target="tpu_custom_call" | custom-call | tf_op jit(solution)/shard_map/pallas_call | solution.py:279
  87.4 0.7 copy.16
  88.0 7.0 %copy.17 = f32[2,58,8192]{2,0,1:T(2,128)} copy(f32[2,58,8192]{2,1,0:T(8,128)} %get-tuple-element.11) | data formatting | bytes 7602176
  (2 shorter events, 0.0 us)
Async XLA Ops:
  0.6 3.7 %copy-start.1 = (s32[128]{0:T(128)S(1)}, s32[128]{0:T(128)}, u32[]{:S(2)}) copy-start(s32[128]{0:T(128)} %param.6) | copy-start | bytes 1540
  0.6 3.7 %copy-start = (f32[3,58,128]{2,1,0:T(8,128)S(1)}, f32[3,58,128]{2,1,0:T(8,128)}, u32[]{:S(2)}) copy-start(f32[3,58,128]{2,1,0:T(8,128)} %gcm_ref.1) | copy-start | bytes 267268
where the time goes:
time: 95.2 us; the launch traced here: 95 us
  Pallas kernels  83 us (87%)
  local copies, waits for them, and re-layouts  10.5 us (11%)
    pallas_call x1, Pallas kernels, on_device(): pl.pallas_call(step_kernel, out_shape=(jax.ShapeDtypeStruct((2, LEV, 8192...  83 us
    unnamed x7, local copies, waits for them, and re-layouts  10.3 us

commit v1 on v0

--- a/solution.py
+++ b/solution.py
@@ -14,6 +14,7 @@
 NX = 4
 NY = 32
 GROUPS = 32
+GROUP = 4
 F32 = jnp.float32
 BF16 = jnp.bfloat16
 MESH = pl.DeviceIdType.MESH
@@ -21,14 +22,16 @@
 NN = (((1,), (0,)), ((), ()))
 NT = (((1,), (1,)), ((), ()))
 
-OFFSETS = [(a, b, c) for a in range(4) for b in range(4) for c in range(2) if (a, b, c) != (0, 0, 0)]
-ORDER = [29, 12, 4, 23, 17, 8, 26, 1, 14, 20, 6, 30, 10, 3, 25, 16, 22, 9, 0, 27, 13, 18, 5, 24, 11, 2, 28, 19, 7, 15, 21]
-
-
-def shifted(gy, offset):
-    dz, dy, dc = offset
-    z, y, c = gy // 8, (gy // 2) % 4, gy % 2
-    return (((z + dz) % 4) * 4 + (y + dy) % 4) * 2 + (c + dc) % 2
+RAW = 16
+WAVES = (3, 10, RAW)
+STRIDE = 13
+
+
+def peer(gy, i, sign):
+    offset = (STRIDE * (i + 1)) % NY
+    z = (gy // 8 + 4 + sign * (offset // 8)) % 4
+    y = ((gy // 2) % 4 + 4 + sign * ((offset // 2) % 4)) % 4
+    return (z * 4 + y) * 2 + (gy + offset) % 2
 
 
 def split(x, pieces):
@@ -70,15 +73,21 @@
 
 
 def step_kernel(
-    slot_ref, source_ref, gcm_ref, crm_hbm,
+    slot_ref, lane_ref, source_hbm, gcm_hbm, crm_hbm,
     out_ref, tend_ref,
-    crm, gpad, x1s, x1r, x2s, x2r, r1s, r1r, r2s, r2r, spread, spread_of, fin, warm, send, mean_sc, coef,
-    crm_sem, own_sem, s1, v1, s2, v2, s3, v3, s4, v4, s5, v5,
+    crm, groups, gcm, source_of, gpad, x1s, x1r, x2s, x2r, r1s, r1r, r2s, r2r, spread, spread_of, fin, warm, send, mean_sc, coef, c6s, c6r,
+    crm_sem, gcm_sem, source_sem, own_sem, s1, v1, s2, v2, s3, v3, s4, v4, s5, v5, s6, v6,
 ):
     gx = lax.axis_index("gx")
     gy = lax.axis_index("gy")
     peers_x = [(gx + d) % NX for d in (1, 2, 3)]
-    peers_y = [shifted(gy, OFFSETS[i]) for i in ORDER]
+    peers_y = [peer(gy, i, 1) for i in range(NY - 1)]
+    gcm_load = pltpu.make_async_copy(gcm_hbm, gcm, gcm_sem)
+    gcm_load.start()
+    source_load = pltpu.make_async_copy(source_hbm, source_of, source_sem)
+    source_load.start()
+    load = pltpu.make_async_copy(crm_hbm, crm, crm_sem)
+    load.start()
 
     barrier = pltpu.get_barrier_semaphore()
     for tx in peers_x:
@@ -86,12 +95,11 @@
     for ty in peers_y:
         pl.semaphore_signal(barrier, inc=1, device_id={"gy": ty}, device_id_type=MESH)
 
-    load = pltpu.make_async_copy(crm_hbm, crm, crm_sem)
-    load.start()
-
     gpad[...] = jnp.zeros((4, PAD, LANES), F32)
-    gpad[0:3, 0:LEV, :] = gcm_ref[...]
-    source = source_ref[...]
+    gcm_load.wait()
+    source_load.wait()
+    gpad[0:3, 0:LEV, :] = gcm[...]
+    source = source_of[...]
     chosen = hot(iota((LANES, LANES), 0) == source)
     packed = pick(gpad[...].reshape(4 * PAD, LANES), chosen)
     x1s[0] = packed[0:128].T
@@ -110,6 +118,41 @@
         copy.start()
         stage1.append(copy)
     x1r[:, own_rows, :] = x1s[:, own_rows, :]
+
+    own_lanes = pl.ds(pl.multiple_of(gy * 256, 256), 256)
+
+    def state_copy(i):
+        return pltpu.make_async_remote_copy(
+            src_ref=send.at[i], dst_ref=out_ref.at[:, :, own_lanes],
+            send_sem=s5.at[i], recv_sem=v5.at[i], device_id={"gy": peer(gy, i, 1)}, device_id_type=MESH,
+        )
+
+    def coef_copy(i):
+        return pltpu.make_async_remote_copy(
+            src_ref=c6s.at[peer(gy, i, 1)], dst_ref=c6r.at[i],
+            send_sem=s6.at[i], recv_sem=v6.at[i], device_id={"gy": peer(gy, i, 1)}, device_id_type=MESH,
+        )
+
+    def send_raw(i, carry):
+        d = peer(gy, i, 1)
+        for r in range(2):
+            g = slot_ref[d * 2 + r]
+            block = groups[jnp.maximum(g, 0)]
+            block = jnp.where(g >= 0, block, 0.0)
+            for f in range(2):
+                send[i, :, f, r * LANES:(r + 1) * LANES] = block[f]
+        state_copy(i).start()
+        return carry
+
+    load.wait()
+
+    def by_group(g, carry):
+        lanes = pl.ds(pl.multiple_of(g * LANES, LANES), LANES)
+        for f in range(2):
+            groups[g, f] = crm[:, f, lanes]
+        return carry
+    lax.fori_loop(0, GROUPS, by_group, 0)
+    lax.fori_loop(0, WAVES[0], send_raw, 0)
 
     def fill(g, carry):
         cols = g * 4 + iota((LANES, LANES), 1) // CRM_X
@@ -134,14 +177,15 @@
         stage2.append(copy)
     x2r[gy] = x2s[gy]
 
-    load.wait()
-
-    def column_means(ref_a, ref_b, out_ref):
+    lax.fori_loop(WAVES[0], WAVES[1], send_raw, 0)
+
+
+    def column_means(read, out_ref):
         out_ref[...] = jnp.zeros((2 * PAD, LANES), F32)
 
         def add(i, carry):
             lanes = pl.ds(pl.multiple_of(i * 512, 512), 512)
-            both = jnp.concatenate([padded(ref_a[:, lanes]), padded(ref_b[:, lanes])], axis=0)
+            both = jnp.concatenate([padded(read(0, lanes)), padded(read(1, lanes))], axis=0)
             hi, lo = split(both, 2)
             e = spread_of[:, lanes]
             out_ref[...] += dot(hi, e, NT) + dot(lo, e, NT)
@@ -150,7 +194,7 @@
         return out_ref[...] * (1.0 / CRM_X)
 
     level = iota((PAD, LANES), 0)
-    means = column_means(crm.at[0], crm.at[1], mean_sc)
+    means = column_means(lambda f, lanes: crm[:, f, lanes], mean_sc)
 
     def below(s):
         return jnp.where(level == 0, s, pltpu.roll(s, 1, 0))
@@ -170,15 +214,24 @@
     wind = pick(landed[0:PAD], perm[1])
     target = [first[0:PAD], first[PAD:128]]
     columns = jnp.concatenate(
-        [0.125 * jnp.tanh(wind)] + [0.5 * (target[f] - moved_mean[f]) for f in range(2)], axis=0)
+        [0.125 * jnp.tanh(wind)] + [0.5 * (target[f] - moved_mean[f]) for f in range(2)]
+        + [jnp.ones((PAD, LANES), F32)], axis=0)
     hi, lo = split(columns, 2)
     coef[0] = hi
     coef[1] = lo
+    to_slot = hot(iota((LANES, 256), 0) == lane_ref[...])
+    c6s[...] = pick(columns, to_slot).T.reshape(NY, 8, 256)
+
+    def send_coef(i, carry):
+        coef_copy(i).start()
+        return carry
+    lax.fori_loop(0, RAW, send_coef, 0)
+    lax.fori_loop(WAVES[1], WAVES[2], send_raw, 0)
 
     def spread_out(i, carry):
         lanes = pl.ds(pl.multiple_of(i * 512, 512), 512)
         e = spread_of[:, lanes]
-        spread[:, lanes] = dot(coef[0], e, NN) + dot(coef[1], e, NN)
+        spread[:, lanes] = dot(coef[0, 0:3 * PAD], e, NN) + dot(coef[1, 0:3 * PAD], e, NN)
         return carry
     lax.fori_loop(0, 8, spread_out, 0)
 
@@ -189,16 +242,20 @@
         east = jnp.where(x == CRM_X - 1, pltpu.roll(s, 31, 1), pltpu.roll(s, LANES - 1, 1))
         return (0.6 * s + 0.1 * ((east + west) + (below(s) + above(s))) - speed * (east - west)) + shift
 
-    def one_group(g, carry):
-        lanes = pl.ds(pl.multiple_of(g * LANES, LANES), LANES)
-        speed = spread[0:PAD, lanes]
-        energy = advance(padded(crm[0, :, lanes]), speed, spread[PAD:2 * PAD, lanes])
-        water = advance(padded(crm[1, :, lanes]), speed, spread[2 * PAD:3 * PAD, lanes])
+    def physics(s0, s1, speed, shift0, shift1):
+        energy = advance(padded(s0), speed, shift0)
+        water = advance(padded(s1), speed, shift1)
         base = 0.5 * energy + (1.25 * water - 0.625)
         half = base - 0.625 * jnp.tanh(0.5 * energy)
         half = base - 0.625 * jnp.tanh(half)
         half = base - 0.625 * jnp.tanh(half)
-        final = 0.8 * water + (0.1 + 0.1 * jnp.tanh(half))
+        return energy, 0.8 * water + (0.1 + 0.1 * jnp.tanh(half)), half
+
+    def one_group(g, carry):
+        lanes = pl.ds(pl.multiple_of(g * LANES, LANES), LANES)
+        energy, final, half = physics(
+            groups[g, 0], groups[g, 1],
+            spread[0:PAD, lanes], spread[PAD:2 * PAD, lanes], spread[2 * PAD:3 * PAD, lanes])
         warm[0, :, lanes] = half + half
         warm[1, :, lanes] = final
         fin[g, 0] = energy[0:LEV]
@@ -206,7 +263,7 @@
         return carry
     lax.fori_loop(0, GROUPS, one_group, 0)
 
-    ends = column_means(warm.at[0], warm.at[1], mean_sc)
+    ends = column_means(lambda f, lanes: warm[f, :, lanes], mean_sc)
     tendency = ends - first
     back = hot((row // 8 == col % 32) & (row % 8 == col // 32))
     r1s[...] = pick_rows(back, tendency, NT).reshape(32, 8, LANES)
@@ -224,21 +281,39 @@
         for r in range(2):
             g = slot_ref[d * 2 + r]
             block = fin[jnp.maximum(g, 0)]
-            send[i, :, :, r * LANES:(r + 1) * LANES] = jnp.where(g >= 0, block, 0.0)
-
-    own_lanes = pl.ds(pl.multiple_of(gy * 256, 256), 256)
-    moves = []
-    for i, ty in enumerate(peers_y):
-        gather(i, ty)
-        copy = pltpu.make_async_remote_copy(
-            src_ref=send.at[i], dst_ref=out_ref.at[:, :, own_lanes],
-            send_sem=s5.at[i], recv_sem=v5.at[i], device_id={"gy": ty}, device_id_type=MESH,
-        )
-        copy.start()
-        moves.append(copy)
+            block = jnp.where(g >= 0, block, 0.0)
+            for f in range(2):
+                send[i, :, f, r * LANES:(r + 1) * LANES] = block[f]
+
+    def send_final(i, carry):
+        gather(i, peer(gy, i, 1))
+        state_copy(i).start()
+        return carry
+    lax.fori_loop(RAW, NY - 1, send_final, 0)
     gather(31, gy)
     own = pltpu.make_async_copy(send.at[31], out_ref.at[:, :, own_lanes], own_sem)
     own.start()
+
+    def wait_coef(i, carry):
+        coef_copy(i).wait()
+        return carry
+    lax.fori_loop(0, RAW, wait_coef, 0)
+    came = split(c6r[...].reshape(RAW * 8, 256).T, 2)
+
+    def finish(i, carry):
+        state_copy(i).wait()
+        e = hot(iota((RAW * 8, 256), 0) == i * 8 + iota((RAW * 8, 256), 1) // CRM_X)
+        both = dot(came[0], e, NN) + dot(came[1], e, NN)
+        start = peer(gy, i, -1) * 256
+        for r in range(2):
+            c = both[:, r * LANES:(r + 1) * LANES]
+            lanes = pl.ds(pl.multiple_of(start + r * LANES, LANES), LANES)
+            energy, final, _ = physics(
+                out_ref[:, 0, lanes], out_ref[:, 1, lanes], c[0:PAD], c[PAD:2 * PAD], c[2 * PAD:3 * PAD])
+            out_ref[:, 0, lanes] = energy[0:LEV]
+            out_ref[:, 1, lanes] = (c[3 * PAD:] * final)[0:LEV]
+        return carry
+    lax.fori_loop(0, RAW, finish, 0)
 
     for copy in stage3:
         copy.wait()
@@ -257,12 +332,15 @@
     for copy in stage4:
         copy.wait()
     placed = pick(r2r[...].T, chosen, NT)
-    tend_ref[0] = placed[0:LEV]
-    tend_ref[1] = placed[PAD:PAD + LEV]
+    tend_ref[:, 0, :] = placed[0:LEV]
+    tend_ref[:, 1, :] = placed[PAD:PAD + LEV]
 
     own.wait()
-    for copy in moves:
-        copy.wait()
+
+    def wait_final(i, carry):
+        state_copy(i).wait()
+        return carry
+    lax.fori_loop(RAW, NY - 1, wait_final, 0)
 
 
 def slots_of(group_owner):
@@ -276,31 +354,31 @@
 def on_device(gcm_state, crm_state, send_source, group_owner):
     vm = pltpu.VMEM
     dma = pltpu.SemaphoreType.DMA
+    slots = slots_of(group_owner)
+    lane = (slots[:, None] * GROUP + jnp.arange(GROUP, dtype=jnp.int32)[None, :]).reshape(1, 256)
+    hbm = pl.BlockSpec(memory_space=pltpu.HBM)
+    vmem = pl.BlockSpec(memory_space=pltpu.VMEM)
     crm_next, tendency = pl.pallas_call(
         step_kernel,
-        out_shape=(jax.ShapeDtypeStruct((2, LEV, 8192), F32), jax.ShapeDtypeStruct((2, LEV, LANES), F32)),
-        in_specs=[
-            pl.BlockSpec(memory_space=pltpu.SMEM),
-            pl.BlockSpec(memory_space=pltpu.VMEM),
-            pl.BlockSpec(memory_space=pltpu.VMEM),
-            pl.BlockSpec(memory_space=pl.ANY),
-        ],
-        out_specs=(pl.BlockSpec(memory_space=pl.ANY), pl.BlockSpec(memory_space=pltpu.VMEM)),
+        out_shape=(jax.ShapeDtypeStruct((LEV, 2, 8192), F32), jax.ShapeDtypeStruct((LEV, 2, LANES), F32)),
+        in_specs=[pl.BlockSpec(memory_space=pltpu.SMEM), vmem, hbm, hbm, hbm],
+        out_specs=(vmem, vmem),
         scratch_shapes=[
-            vm((2, LEV, 4096), F32), vm((4, PAD, LANES), F32),
+            vm((LEV, 2, 4096), F32), vm((GROUPS, 2, LEV, LANES), F32), vm((3, LEV, LANES), F32), vm((1, LANES), jnp.int32), vm((4, PAD, LANES), F32),
             vm((2, 128, LANES), F32), vm((2, 128, LANES), F32),
             vm((32, 8, LANES), F32), vm((32, 8, LANES), F32),
             vm((32, 8, LANES), F32), vm((32, 8, LANES), F32),
             vm((128, LANES), F32), vm((128, LANES), F32),
             vm((3 * PAD, 4096), F32), vm((LANES, 4096), BF16),
             vm((GROUPS, 2, LEV, LANES), F32), vm((2, PAD, 4096), F32),
-            vm((32, 2, LEV, 256), F32), vm((2 * PAD, LANES), F32), vm((2, 3 * PAD, LANES), BF16),
-            dma, dma, dma((3,)), dma((3,)), dma((31,)), dma((31,)), dma((31,)), dma((31,)),
-            dma((3,)), dma((3,)), dma((31,)), dma((31,)),
+            vm((32, LEV, 2, 256), F32), vm((2 * PAD, LANES), F32), vm((2, 4 * PAD, LANES), BF16),
+            vm((NY, 8, 256), F32), vm((RAW, 8, 256), F32),
+            dma, dma, dma, dma, dma((3,)), dma((3,)), dma((31,)), dma((31,)), dma((31,)), dma((31,)),
+            dma((3,)), dma((3,)), dma((31,)), dma((31,)), dma((RAW,)), dma((RAW,)),
         ],
         compiler_params=pltpu.CompilerParams(collective_id=0, has_side_effects=True, vmem_limit_bytes=48 << 20),
-    )(slots_of(group_owner), send_source.reshape(1, LANES), gcm_state, crm_state)
-    return tendency, crm_next
+    )(slots, lane, send_source.reshape(1, LANES), gcm_state, crm_state.transpose(1, 0, 2))
+    return tendency.transpose(1, 0, 2), crm_next.transpose(1, 0, 2)
 
 
 def solution(mesh):

time: 95.2 us -> 72.3 us (0.76)
  Pallas kernels: 83 us -> 64.7 us
  local copies, waits for them, and re-layouts: 10.5 us -> 5.87 us
    pallas_call x1, Pallas kernels: 83 us -> 64.7 us  [on_device(): pl.pallas_call(step_kernel, out_shape=(jax.ShapeDtypeStruct((LEV, 2, 8192...]
    unnamed x7 -> x8, local copies, waits for them, and re-layouts: 10.3 us -> 5.57 us
where the time goes in v1:
time: 72.3 us; the launch traced here: 72.1 us
  Pallas kernels  64.7 us (89%)
  local copies, waits for them, and re-layouts  5.87 us (8%)
  other arithmetic  0.87 us (1%)
    pallas_call x1, Pallas kernels, on_device(): pl.pallas_call(step_kernel, out_shape=(jax.ShapeDtypeStruct((LEV, 2, 8192...  64.7 us
    unnamed x8, local copies, waits for them, and re-layouts  5.57 us

profile of v1, /device:TPU:1, one launch (start us, length us, event | category | flops | bytes accessed | tf_op | source)
XLA Modules:
  0.0 72.1 jit_solution(10638950627945302789)
XLA Ops:
  0.6 0.8 %select_reduce_fusion.1 = (s32[32]{0:T(128)S(1)}, s32[32]{0:T(128)S(1)}) fusion(s32[32]{0:T(128)} %param.7), kind=kLoop, calls=%fused_computation.2 | loop fusion | flops 5056 | bytes 384 | tf_op jit(solution)/shard_map/reduce_max | solution.py:350
  1.4 0.1 copy.8
  1.5 0.1 reshape.69.slot_ref
  1.6 0.1 iota_add_fusion
  1.7 0.1 add.26.lane_ref
  1.8 0.0 copy-start
  1.8 1.5 %copy-done = f32[2,58,4096]{2,0,1:T(2,128)S(1)} copy-done((f32[2,58,4096]{2,0,1:T(2,128)S(1)}, f32[2,58,4096]{2,0,1:T(2,128)}, u32[]{:S(2)}) %copy-start) | copy-done | bytes 1900568
  3.4 0.0 copy-start.1
  3.4 0.9 %copy-done.1 = f32[3,58,128]{2,1,0:T(8,128)S(1)} copy-done((f32[3,58,128]{2,1,0:T(8,128)S(1)}, f32[3,58,128]{2,1,0:T(8,128)}, u32[]{:S(2)}) %copy-start.1) | copy-done | bytes 89112
  4.2 0.0 copy-start.2
  4.2 0.7 copy-done.2
  4.9 64.7 %shard_map.59 = (f32[58,2,8192]{2,1,0:T(2,128)S(1)}, f32[58,2,128]{2,1,0:T(2,128)S(1)}) custom-call(s32[64]{0:T(128)S(1)} %reshape.69.slot_ref, s32[1,256]{1,0:T(1,128)S(1)} %add.26.lane_ref, s32[1,128]{1,0:T(1,128)S(1)} %bitcast.13, f32[3,58,128]{2,1,0:T(8,128)S(1)} %copy-done.1, f32[58,2,4096]{2,1,0:T(2,128)S(1)} %bitcast.11), custom_call_target="tpu_custom_call" | custom-call | tf_op jit(solution)/shard_map/pallas_call | solution.py:361
  69.6 0.6 copy.11
  70.2 1.9 %copy.12 = f32[2,58,8192]{2,0,1:T(2,128)} copy(f32[2,58,8192]{2,0,1:T(2,128)S(1)} %bitcast.10) | data formatting | bytes 7602176
  (3 shorter events, 0.0 us)
Async XLA Ops:
  1.8 1.5 %copy-start = (f32[2,58,4096]{2,0,1:T(2,128)S(1)}, f32[2,58,4096]{2,0,1:T(2,128)}, u32[]{:S(2)}) copy-start(f32[2,58,4096]{2,0,1:T(2,128)} %param.5) | copy-start | bytes 5701636
  3.4 0.9 %copy-start.1 = (f32[3,58,128]{2,1,0:T(8,128)S(1)}, f32[3,58,128]{2,1,0:T(8,128)}, u32[]{:S(2)}) copy-start(f32[3,58,128]{2,1,0:T(8,128)} %gcm_hbm.1) | copy-start | bytes 267268
  4.2 0.7 copy-start.2

commit v2 on v1

--- a/solution.py
+++ b/solution.py
@@ -23,7 +23,7 @@
 NT = (((1,), (1,)), ((), ()))
 
 RAW = 16
-WAVES = (3, 10, RAW)
+WAVES = (4, 10, RAW)
 STRIDE = 13
 
 
@@ -73,15 +73,17 @@
 
 
 def step_kernel(
-    slot_ref, lane_ref, source_hbm, gcm_hbm, crm_hbm,
+    owner_hbm, source_hbm, gcm_hbm, crm_hbm,
     out_ref, tend_ref,
-    crm, groups, gcm, source_of, gpad, x1s, x1r, x2s, x2r, r1s, r1r, r2s, r2r, spread, spread_of, fin, warm, send, mean_sc, coef, c6s, c6r,
-    crm_sem, gcm_sem, source_sem, own_sem, s1, v1, s2, v2, s3, v3, s4, v4, s5, v5, s6, v6,
+    crm, groups, gcm, source_of, gpad, x1s, x1r, x2s, x2r, r1s, r1r, r2s, r2r, spread, spread_of, fin, warm, send, mean_sc, coef, c6s, c6r, coef_rows,
+    owner, crm_sem, owner_sem, gcm_sem, source_sem, own_sem, s1, v1, s2, v2, s3, v3, s4, v4, s5, v5, s6, v6,
 ):
     gx = lax.axis_index("gx")
     gy = lax.axis_index("gy")
     peers_x = [(gx + d) % NX for d in (1, 2, 3)]
     peers_y = [peer(gy, i, 1) for i in range(NY - 1)]
+    owner_load = pltpu.make_async_copy(owner_hbm, owner, owner_sem)
+    owner_load.start()
     gcm_load = pltpu.make_async_copy(gcm_hbm, gcm, gcm_sem)
     gcm_load.start()
     source_load = pltpu.make_async_copy(source_hbm, source_of, source_sem)
@@ -94,6 +96,52 @@
         pl.semaphore_signal(barrier, inc=1, device_id={"gx": tx}, device_id_type=MESH)
     for ty in peers_y:
         pl.semaphore_signal(barrier, inc=1, device_id={"gy": ty}, device_id_type=MESH)
+
+    own_lanes = pl.ds(pl.multiple_of(gy * 256, 256), 256)
+
+    def state_copy(i):
+        return pltpu.make_async_remote_copy(
+            src_ref=send.at[i], dst_ref=out_ref.at[:, :, own_lanes],
+            send_sem=s5.at[i], recv_sem=v5.at[i], device_id={"gy": peer(gy, i, 1)}, device_id_type=MESH,
+        )
+
+    def coef_copy(i):
+        return pltpu.make_async_remote_copy(
+            src_ref=c6s.at[i], dst_ref=c6r.at[i],
+            send_sem=s6.at[i], recv_sem=v6.at[i], device_id={"gy": peer(gy, i, 1)}, device_id_type=MESH,
+        )
+
+    def slots_for(d):
+        low, high = jnp.int32(GROUPS), jnp.int32(-1)
+        for g in range(GROUPS):
+            same = owner[g] == d
+            low = jnp.minimum(low, jnp.where(same, g, GROUPS))
+            high = jnp.where(same, g, high)
+        return jnp.where(high < 0, -1, low), jnp.where(high > low, high, -1)
+
+    def gather(i, d, blocks):
+        for r, g in enumerate(slots_for(d)):
+            block = blocks[jnp.maximum(g, 0)]
+            block = jnp.where(g >= 0, block, 0.0)
+            for f in range(2):
+                send[i, :, f, r * LANES:(r + 1) * LANES] = block[f]
+
+    def send_raw(i, carry):
+        gather(i, peer(gy, i, 1), groups)
+        state_copy(i).start()
+        return carry
+
+    load.wait()
+    owner_load.wait()
+
+    def by_group(g, carry):
+        lanes = pl.ds(pl.multiple_of(g * LANES, LANES), LANES)
+        for f in range(2):
+            groups[g, f] = crm[:, f, lanes]
+        return carry
+    lax.fori_loop(0, GROUPS, by_group, 0)
+    pl.semaphore_wait(barrier, 3 + 31)
+    lax.fori_loop(0, WAVES[0], send_raw, 0)
 
     gpad[...] = jnp.zeros((4, PAD, LANES), F32)
     gcm_load.wait()
@@ -105,8 +153,6 @@
     x1s[0] = packed[0:128].T
     x1s[1] = packed[128:256].T
 
-    pl.semaphore_wait(barrier, 3 + 31)
-
     own_rows = pl.ds(pl.multiple_of(gx * 32, 32), 32)
     stage1 = []
     for i, tx in enumerate(peers_x):
@@ -119,40 +165,6 @@
         stage1.append(copy)
     x1r[:, own_rows, :] = x1s[:, own_rows, :]
 
-    own_lanes = pl.ds(pl.multiple_of(gy * 256, 256), 256)
-
-    def state_copy(i):
-        return pltpu.make_async_remote_copy(
-            src_ref=send.at[i], dst_ref=out_ref.at[:, :, own_lanes],
-            send_sem=s5.at[i], recv_sem=v5.at[i], device_id={"gy": peer(gy, i, 1)}, device_id_type=MESH,
-        )
-
-    def coef_copy(i):
-        return pltpu.make_async_remote_copy(
-            src_ref=c6s.at[peer(gy, i, 1)], dst_ref=c6r.at[i],
-            send_sem=s6.at[i], recv_sem=v6.at[i], device_id={"gy": peer(gy, i, 1)}, device_id_type=MESH,
-        )
-
-    def send_raw(i, carry):
-        d = peer(gy, i, 1)
-        for r in range(2):
-            g = slot_ref[d * 2 + r]
-            block = groups[jnp.maximum(g, 0)]
-            block = jnp.where(g >= 0, block, 0.0)
-            for f in range(2):
-                send[i, :, f, r * LANES:(r + 1) * LANES] = block[f]
-        state_copy(i).start()
-        return carry
-
-    load.wait()
-
-    def by_group(g, carry):
-        lanes = pl.ds(pl.multiple_of(g * LANES, LANES), LANES)
-        for f in range(2):
-            groups[g, f] = crm[:, f, lanes]
-        return carry
-    lax.fori_loop(0, GROUPS, by_group, 0)
-    lax.fori_loop(0, WAVES[0], send_raw, 0)
 
     def fill(g, carry):
         cols = g * 4 + iota((LANES, LANES), 1) // CRM_X
@@ -213,16 +225,20 @@
     first = pick(landed, perm[0])
     wind = pick(landed[0:PAD], perm[1])
     target = [first[0:PAD], first[PAD:128]]
-    columns = jnp.concatenate(
-        [0.125 * jnp.tanh(wind)] + [0.5 * (target[f] - moved_mean[f]) for f in range(2)]
-        + [jnp.ones((PAD, LANES), F32)], axis=0)
+    speeds = jnp.where(level == PAD - 1, 1.0, 0.125 * jnp.tanh(wind))
+    columns = jnp.concatenate([speeds] + [0.5 * (target[f] - moved_mean[f]) for f in range(2)], axis=0)
     hi, lo = split(columns, 2)
     coef[0] = hi
     coef[1] = lo
-    to_slot = hot(iota((LANES, 256), 0) == lane_ref[...])
-    c6s[...] = pick(columns, to_slot).T.reshape(NY, 8, 256)
+    col256 = iota((LANES, 256), 1)
+    twice = hot(iota((LANES, 256), 0) == (col256 // 8) * GROUP + col256 % GROUP)
+    coef_rows[...] = pick(columns, twice).T.reshape(GROUPS, 8, 3 * PAD)
 
     def send_coef(i, carry):
+        g, h = slots_for(peer(gy, i, 1))
+        first_half = jnp.where(g >= 0, coef_rows[jnp.maximum(g, 0)], 0.0)
+        second_half = jnp.where(h >= 0, coef_rows[jnp.maximum(h, 0)], 0.0)
+        c6s[i] = jnp.where(iota((8, 3 * PAD), 0) < GROUP, first_half, second_half)
         coef_copy(i).start()
         return carry
     lax.fori_loop(0, RAW, send_coef, 0)
@@ -231,7 +247,7 @@
     def spread_out(i, carry):
         lanes = pl.ds(pl.multiple_of(i * 512, 512), 512)
         e = spread_of[:, lanes]
-        spread[:, lanes] = dot(coef[0, 0:3 * PAD], e, NN) + dot(coef[1, 0:3 * PAD], e, NN)
+        spread[:, lanes] = dot(coef[0], e, NN) + dot(coef[1], e, NN)
         return carry
     lax.fori_loop(0, 8, spread_out, 0)
 
@@ -266,7 +282,7 @@
     ends = column_means(lambda f, lanes: warm[f, :, lanes], mean_sc)
     tendency = ends - first
     back = hot((row // 8 == col % 32) & (row % 8 == col // 32))
-    r1s[...] = pick_rows(back, tendency, NT).reshape(32, 8, LANES)
+    r1s[...] = pick_rows(back, tendency, NT).reshape(32, 8, LANES)[:, 0:NX]
     stage3 = []
     for i, ty in enumerate(peers_y):
         copy = pltpu.make_async_remote_copy(
@@ -277,20 +293,12 @@
         stage3.append(copy)
     r1r[gy] = r1s[gy]
 
-    def gather(i, d):
-        for r in range(2):
-            g = slot_ref[d * 2 + r]
-            block = fin[jnp.maximum(g, 0)]
-            block = jnp.where(g >= 0, block, 0.0)
-            for f in range(2):
-                send[i, :, f, r * LANES:(r + 1) * LANES] = block[f]
-
     def send_final(i, carry):
-        gather(i, peer(gy, i, 1))
+        gather(i, peer(gy, i, 1), fin)
         state_copy(i).start()
         return carry
     lax.fori_loop(RAW, NY - 1, send_final, 0)
-    gather(31, gy)
+    gather(31, gy, fin)
     own = pltpu.make_async_copy(send.at[31], out_ref.at[:, :, own_lanes], own_sem)
     own.start()
 
@@ -298,7 +306,7 @@
         coef_copy(i).wait()
         return carry
     lax.fori_loop(0, RAW, wait_coef, 0)
-    came = split(c6r[...].reshape(RAW * 8, 256).T, 2)
+    came = split(c6r[...].reshape(RAW * 8, 3 * PAD).T, 2)
 
     def finish(i, carry):
         state_copy(i).wait()
@@ -311,7 +319,7 @@
             energy, final, _ = physics(
                 out_ref[:, 0, lanes], out_ref[:, 1, lanes], c[0:PAD], c[PAD:2 * PAD], c[2 * PAD:3 * PAD])
             out_ref[:, 0, lanes] = energy[0:LEV]
-            out_ref[:, 1, lanes] = (c[3 * PAD:] * final)[0:LEV]
+            out_ref[:, 1, lanes] = (c[PAD - 1:PAD] * final)[0:LEV]
         return carry
     lax.fori_loop(0, RAW, finish, 0)
 
@@ -319,7 +327,9 @@
         copy.wait()
     rows = iota((LANES, 256), 0)
     cols = iota((LANES, 256), 1)
-    r2s[...] = pick_rows(hot((rows % 32 == cols // 8) & (rows // 32 == cols % 8)), r1r[...].reshape(256, LANES))
+    r2s[...] = pick_rows(
+        hot((rows % 32 == cols // 8) & (rows // 32 == cols % 8)),
+        jnp.concatenate([r1r[...], jnp.zeros((NY, 8 - NX, LANES), F32)], axis=1).reshape(256, LANES))
     stage4 = []
     for i, tx in enumerate(peers_x):
         copy = pltpu.make_async_remote_copy(
@@ -343,41 +353,32 @@
     lax.fori_loop(RAW, NY - 1, wait_final, 0)
 
 
-def slots_of(group_owner):
-    g = jnp.arange(GROUPS, dtype=jnp.int32)[None, :]
-    same = group_owner[None, :] == jnp.arange(NY, dtype=jnp.int32)[:, None]
-    low = jnp.min(jnp.where(same, g, GROUPS), axis=1)
-    high = jnp.max(jnp.where(same, g, -1), axis=1)
-    return jnp.stack([jnp.where(high < 0, -1, low), jnp.where(high > low, high, -1)], axis=1).reshape(2 * NY)
-
-
 def on_device(gcm_state, crm_state, send_source, group_owner):
     vm = pltpu.VMEM
     dma = pltpu.SemaphoreType.DMA
-    slots = slots_of(group_owner)
-    lane = (slots[:, None] * GROUP + jnp.arange(GROUP, dtype=jnp.int32)[None, :]).reshape(1, 256)
     hbm = pl.BlockSpec(memory_space=pltpu.HBM)
     vmem = pl.BlockSpec(memory_space=pltpu.VMEM)
     crm_next, tendency = pl.pallas_call(
         step_kernel,
         out_shape=(jax.ShapeDtypeStruct((LEV, 2, 8192), F32), jax.ShapeDtypeStruct((LEV, 2, LANES), F32)),
-        in_specs=[pl.BlockSpec(memory_space=pltpu.SMEM), vmem, hbm, hbm, hbm],
+        in_specs=[hbm] * 4,
         out_specs=(vmem, vmem),
         scratch_shapes=[
             vm((LEV, 2, 4096), F32), vm((GROUPS, 2, LEV, LANES), F32), vm((3, LEV, LANES), F32), vm((1, LANES), jnp.int32), vm((4, PAD, LANES), F32),
             vm((2, 128, LANES), F32), vm((2, 128, LANES), F32),
             vm((32, 8, LANES), F32), vm((32, 8, LANES), F32),
-            vm((32, 8, LANES), F32), vm((32, 8, LANES), F32),
+            vm((32, NX, LANES), F32), vm((32, NX, LANES), F32),
             vm((128, LANES), F32), vm((128, LANES), F32),
             vm((3 * PAD, 4096), F32), vm((LANES, 4096), BF16),
             vm((GROUPS, 2, LEV, LANES), F32), vm((2, PAD, 4096), F32),
-            vm((32, LEV, 2, 256), F32), vm((2 * PAD, LANES), F32), vm((2, 4 * PAD, LANES), BF16),
-            vm((NY, 8, 256), F32), vm((RAW, 8, 256), F32),
-            dma, dma, dma, dma, dma((3,)), dma((3,)), dma((31,)), dma((31,)), dma((31,)), dma((31,)),
+            vm((32, LEV, 2, 256), F32), vm((2 * PAD, LANES), F32), vm((2, 3 * PAD, LANES), BF16),
+            vm((RAW, 8, 3 * PAD), F32), vm((RAW, 8, 3 * PAD), F32), vm((GROUPS, 8, 3 * PAD), F32),
+            pltpu.SMEM((GROUPS,), jnp.int32), dma, dma, dma, dma, dma, dma((3,)), dma((3,)), dma((31,)), dma((31,)), dma((31,)), dma((31,)),
             dma((3,)), dma((3,)), dma((31,)), dma((31,)), dma((RAW,)), dma((RAW,)),
         ],
         compiler_params=pltpu.CompilerParams(collective_id=0, has_side_effects=True, vmem_limit_bytes=48 << 20),
-    )(slots, lane, send_source.reshape(1, LANES), gcm_state, crm_state.transpose(1, 0, 2))
+    )(*[pltpu.with_memory_space_constraint(a, pltpu.HBM) for a in (
+        group_owner, send_source.reshape(1, LANES), gcm_state, crm_state.transpose(1, 0, 2))])
     return tendency.transpose(1, 0, 2), crm_next.transpose(1, 0, 2)
 
 

time: 72.3 us -> 66.7 us (0.923)
  local copies, waits for them, and re-layouts: 5.87 us -> 2.51 us
  Pallas kernels: 64.7 us -> 63.4 us
  other arithmetic: 0.87 us -> 0 us
    unnamed x8 -> x2, local copies, waits for them, and re-layouts: 5.57 us -> 2.51 us
    pallas_call x1, Pallas kernels: 64.7 us -> 63.4 us  [on_device(): pl.pallas_call(step_kernel, out_shape=(jax.ShapeDtypeStruct((LEV, 2, 8192...]
    reduce_max x1 -> x0, other arithmetic: 0.77 us -> none  [slots_of(): high = jnp.max(jnp.where(same, g, -1), axis=1)]
where the time goes in v2:
time: 66.7 us; the launch traced here: 66.6 us
  Pallas kernels  63.4 us (95%)
  local copies, waits for them, and re-layouts  2.51 us (4%)
    pallas_call x1, Pallas kernels, on_device(): pl.pallas_call(step_kernel, out_shape=(jax.ShapeDtypeStruct((LEV, 2, 8192...  63.4 us
    unnamed x2, local copies, waits for them, and re-layouts  2.51 us

profile of v2, /device:TPU:1, one launch (start us, length us, event | category | flops | bytes accessed | tf_op | source)
XLA Modules:
  0.0 66.6 jit_solution(17895415179343388649)
XLA Ops:
  0.6 63.4 %shard_map.59 = (f32[58,2,8192]{2,1,0:T(2,128)S(1)}, f32[58,2,128]{2,1,0:T(2,128)S(1)}) custom-call(s32[32]{0:T(128)} %owner_hbm.1, s32[1,128]{1,0:T(1,128)} %bitcast.7, f32[3,58,128]{2,1,0:T(8,128)} %gcm_hbm.1, f32[58,2,4096]{2,1,0:T(2,128)} %bitcast.6), custom_call_target="tpu_custom_call" | custom-call | tf_op jit(solution)/shard_map/pallas_call | solution.py:361
  64.1 0.6 copy.8
  64.7 1.9 %copy.9 = f32[2,58,8192]{2,0,1:T(2,128)} copy(f32[2,58,8192]{2,0,1:T(2,128)S(1)} %bitcast.4) | data formatting | bytes 7602176

commit v3 on v2

v3 whole, which is shorter than its diff:
```python
import functools

import jax
import jax.numpy as jnp
from jax import lax
from jax.experimental import pallas as pl
from jax.experimental.pallas import tpu as pltpu
from jax.sharding import PartitionSpec as P

CRM_X = 32
LEV = 58
PAD = 64
LANES = 128
NX = 4
NY = 32
GROUPS = 32
GROUP = 4
F32 = jnp.float32
BF16 = jnp.bfloat16
MESH = pl.DeviceIdType.MESH

NN = (((1,), (0,)), ((), ()))
NT = (((1,), (1,)), ((), ()))

RAW = 16
WAVES = (2, 12, RAW, RAW)
STRIDE = 13


def peer(gy, i, sign):
    offset = (STRIDE * (i + 1)) % NY
    other = (gy + offset) % 2
    second = gy % 2 if sign > 0 else other
    dz, dy = offset // 8, (offset // 2) % 4
    step_z = dz * (1 - 2 * second)
    step_y = dy
    z = (gy // 8 + 4 + sign * step_z) % 4
    y = ((gy // 2) % 4 + 4 + sign * step_y) % 4
    return (z * 4 + y) * 2 + other


def split(x, pieces):
    out = []
    for _ in range(pieces - 1):
        hi = x.astype(BF16)
        out.append(hi)
        x = x - hi.astype(F32)
    out.append(x.astype(BF16))
    return out


def dot(a, b, dims):
    return lax.dot_general(a, b, dims, preferred_element_type=F32)


def pick(x, onehot, dims=NN):
    parts = [dot(p, onehot, dims) for p in split(x, 3)]
    return parts[0] + (parts[1] + parts[2])


def pick_rows(onehot, x, dims=NN):
    parts = [dot(onehot, p, dims) for p in split(x, 3)]
    return parts[0] + (parts[1] + parts[2])


def iota(shape, dim):
    return lax.broadcasted_iota(jnp.int32, shape, dim)


def hot(cond):
    return jnp.where(cond, 1.0, 0.0).astype(BF16)


def padded(s):
    if s.shape[0] == PAD:
        return s
    return jnp.concatenate([s, jnp.zeros((PAD - LEV, s.shape[1]), F32)], axis=0)


def step_kernel(
    owner_hbm, source_hbm, gcm_hbm, crm_hbm,
    out_ref, tend_ref,
    crm, gcm, source_of, gpad, x1s, x1r, x2s, x2r, r1s, r1r, r2s, r2r, spread, spread_of, fin, warm, send, mean_sc, coef,
    c6s, c6r, coef_rows, raw,
    owner, crm_sem, owner_sem, gcm_sem, source_sem, own_sem, s1, v1, s2, v2, s3, v3, s4, v4, s5, v5, s6, v6,
):
    gx = lax.axis_index("gx")
    gy = lax.axis_index("gy")
    peers_x = [(gx + d) % NX for d in (1, 2, 3)]

    barrier = pltpu.get_barrier_semaphore()
    for tx in peers_x:
        pl.semaphore_signal(barrier, inc=1, device_id={"gx": tx}, device_id_type=MESH)
    for i in range(NY - 1):
        pl.semaphore_signal(barrier, inc=1, device_id={"gy": peer(gy, i, 1)}, device_id_type=MESH)

    gcm_load = pltpu.make_async_copy(gcm_hbm, gcm, gcm_sem)
    source_load = pltpu.make_async_copy(source_hbm, source_of, source_sem)
    owner_load = pltpu.make_async_copy(owner_hbm, owner, owner_sem)
    gcm_load.start()
    source_load.start()
    owner_load.start()

    def group_load(g):
        lanes = pl.ds(pl.multiple_of(g * LANES, LANES), LANES)
        return pltpu.make_async_copy(crm_hbm.at[:, :, lanes], crm.at[g, pl.ds(1, LEV)], crm_sem.at[g])

    def start_load(g, carry):
        group_load(g).start()
        return carry
    lax.fori_loop(0, GROUPS, start_load, 0)

    gpad[...] = jnp.zeros((4, PAD, LANES), F32)
    gcm_load.wait()
    source_load.wait()
    gpad[0:3, 0:LEV, :] = gcm[...]
    chosen = hot(iota((LANES, LANES), 0) == source_of[...])
    packed = pick(gpad[...].reshape(4 * PAD, LANES), chosen)
    x1s[0] = packed[0:128].T
    x1s[1] = packed[128:256].T
    own_rows = pl.ds(pl.multiple_of(gx * 32, 32), 32)

    pl.semaphore_wait(barrier, 3 + 31)
    stage1 = []
    for i, tx in enumerate(peers_x):
        copy = pltpu.make_async_remote_copy(
            src_ref=x1s.at[:, pl.ds(pl.multiple_of(tx * 32, 32), 32), :],
            dst_ref=x1r.at[:, own_rows, :],
            send_sem=s1.at[i], recv_sem=v1.at[i], device_id={"gx": tx}, device_id_type=MESH,
        )
        copy.start()
        stage1.append(copy)

    own_lanes = pl.ds(pl.multiple_of(gy * 256, 256), 256)

    def state_copy(i):
        return pltpu.make_async_remote_copy(
            src_ref=send.at[i], dst_ref=out_ref.at[:, :, own_lanes],
            send_sem=s5.at[i], recv_sem=v5.at[i], device_id={"gy": peer(gy, i, 1)}, device_id_type=MESH,
        )

    def raw_copy(i):
        return pltpu.make_async_remote_copy(
            src_ref=send.at[i], dst_ref=raw.at[i, pl.ds(1, LEV)],
            send_sem=s5.at[i], recv_sem=v5.at[i], device_id={"gy": peer(gy, i, 1)}, device_id_type=MESH,
        )

    def column_copy(i):
        return pltpu.make_async_remote_copy(
            src_ref=x2s.at[peer(gy, i, 1)], dst_ref=x2r.at[gy],
            send_sem=s2.at[i], recv_sem=v2.at[i], device_id={"gy": peer(gy, i, 1)}, device_id_type=MESH,
        )

    def tendency_copy(i):
        return pltpu.make_async_remote_copy(
            src_ref=r1s.at[peer(gy, i, 1)], dst_ref=r1r.at[gy],
            send_sem=s3.at[i], recv_sem=v3.at[i], device_id={"gy": peer(gy, i, 1)}, device_id_type=MESH,
        )

    def coef_copy(i):
        return pltpu.make_async_remote_copy(
            src_ref=c6s.at[i], dst_ref=c6r.at[i],
            send_sem=s6.at[i], recv_sem=v6.at[i], device_id={"gy": peer(gy, i, 1)}, device_id_type=MESH,
        )

    def slots_for(d):
        low, high = jnp.int32(GROUPS), jnp.int32(-1)
        for g in range(GROUPS):
            same = owner[g] == d
            low = jnp.minimum(low, jnp.where(same, g, GROUPS))
            high = jnp.where(same, g, high)
        return jnp.where(high < 0, -1, low), jnp.where(high > low, high, -1)

    def send_raw(i, carry):
        for r, g in enumerate(slots_for(peer(gy, i, 1))):
            send[i, :, :, r * LANES:(r + 1) * LANES] = jnp.where(g >= 0, crm[jnp.maximum(g, 0)][1:1 + LEV], 0.0)
        raw_copy(i).start()
        return carry

    def wait_load(g, carry):
        group_load(g).wait()
        return carry
    owner_load.wait()
    lax.fori_loop(0, GROUPS, wait_load, 0)
    lax.fori_loop(0, WAVES[0], send_raw, 0)

    def fill(g, carry):
        cols = g * GROUP + iota((LANES, LANES), 1) // CRM_X
        spread_of[:, pl.ds(pl.multiple_of(g * LANES, LANES), LANES)] = hot(iota((LANES, LANES), 0) == cols)
        return carry
    lax.fori_loop(0, GROUPS, fill, 0)
    row = iota((256, LANES), 0)
    col = iota((256, LANES), 1)
    here = (row // 8 == col % 32)
    perm = [hot(here & (row % 8 == (col // 32) * 2 + h)) for h in range(2)]

    x1r[:, own_rows, :] = x1s[:, own_rows, :]
    for copy in stage1:
        copy.wait()
    x2s[...] = (pick_rows(perm[0], x1r[0]) + pick_rows(perm[1], x1r[1])).reshape(32, 8, LANES)
    for i in range(NY - 1):
        column_copy(i).start()
    x2r[gy] = x2s[gy]
    lax.fori_loop(WAVES[0], WAVES[1], send_raw, 0)

    mean_sc[...] = jnp.zeros((2 * PAD, LANES), F32)

    def repeat_ends(ref, i):
        ref[i, 0:1] = ref[i, 1:2]
        ref[i, LEV + 1:LEV + 2] = ref[i, LEV:LEV + 1]

    def add_mean(i, carry):
        total = mean_sc[...]
        for h in range(2):
            g = i * 2 + h
            repeat_ends(crm, g)
            fields = [padded(crm[g, pl.ds(1, LEV), f, :]) for f in range(2)]
            hi, lo = split(jnp.concatenate(fields, axis=0), 2)
            e = spread_of[:, pl.ds(pl.multiple_of(g * LANES, LANES), LANES)]
            total = total + (dot(hi, e, NT) + dot(lo, e, NT))
        mean_sc[...] = total
        return carry
    lax.fori_loop(0, GROUPS // 2, add_mean, 0)
    means = mean_sc[...] * (1.0 / CRM_X)
    level = iota((PAD, LANES), 0)

    def below(s):
        return jnp.where(level == 0, s, pltpu.roll(s, 1, 0))

    def above(s):
        return jnp.where(level == LEV - 1, s, pltpu.roll(s, PAD - 1, 0))

    moved_mean = []
    for f in range(2):
        m = means[f * PAD:(f + 1) * PAD]
        moved_mean.append(0.8 * m + 0.1 * (below(m) + above(m)))

    for i in range(NY - 1):
        column_copy(i).wait()
    landed = x2r[...].reshape(256, LANES).T
    first = pick(landed, perm[0])
    wind = pick(landed[0:PAD], perm[1])
    target = [first[0:PAD], first[PAD:128]]
    speeds = jnp.where(level == PAD - 1, 1.0, 0.125 * jnp.tanh(wind))
    columns = jnp.concatenate([speeds] + [0.5 * (target[f] - moved_mean[f]) for f in range(2)], axis=0)
    hi, lo = split(columns, 2)
    coef[0] = hi
    coef[1] = lo
    col256 = iota((LANES, 256), 1)
    twice = hot(iota((LANES, 256), 0) == (col256 // 8) * GROUP + col256 % GROUP)
    coef_rows[...] = pick(columns, twice).T.reshape(GROUPS, 8, 3 * PAD)

    def send_coef(i, carry):
        g, h = slots_for(peer(gy, i, 1))
        first_half = jnp.where(g >= 0, coef_rows[jnp.maximum(g, 0)], 0.0)
        second_half = jnp.where(h >= 0, coef_rows[jnp.maximum(h, 0)], 0.0)
        c6s[i] = jnp.where(iota((8, 3 * PAD), 0) < GROUP, first_half, second_half)
        coef_copy(i).start()
        return carry
    lax.fori_loop(0, RAW, send_coef, 0)
    lax.fori_loop(WAVES[1], WAVES[2], send_raw, 0)
    x = iota((PAD, LANES), 1) % CRM_X

    def advance(read, speed, shift):
        s = padded(read(1))
        west = jnp.where(x == 0, pltpu.roll(s, LANES - 31, 1), pltpu.roll(s, 1, 1))
        east = jnp.where(x == CRM_X - 1, pltpu.roll(s, 31, 1), pltpu.roll(s, LANES - 1, 1))
        return (0.6 * s + 0.1 * ((east + west) + (padded(read(0)) + padded(read(2)))) - speed * (east - west)) + shift

    def physics(ref, i, lanes, speed, shift0, shift1):
        energy = advance(lambda k: ref[i, pl.ds(k, LEV), 0, lanes], speed, shift0)
        water = advance(lambda k: ref[i, pl.ds(k, LEV), 1, lanes], speed, shift1)
        base = 0.5 * energy + (1.25 * water - 0.625)
        half = base - 0.625 * jnp.tanh(0.5 * energy)
        half = base - 0.625 * jnp.tanh(half)
        half = base - 0.625 * jnp.tanh(half)
        return energy, 0.8 * water + (0.1 + 0.1 * jnp.tanh(half)), half

    def spread_out(i, slot):
        e = spread_of[:, pl.ds(pl.multiple_of(i * 256, 256), 256)]
        spread[slot] = dot(coef[0], e, NN) + dot(coef[1], e, NN)
    spread_out(0, 0)

    def two_groups(i, carry):
        slot = i % 2
        spread_out((i + 1) % (GROUPS // 2), (i + 1) % 2)
        for h in range(2):
            g = i * 2 + h
            c = slice(h * LANES, (h + 1) * LANES)
            energy, final, half = physics(
                crm, g, slice(None),
                spread[slot, 0:PAD, c], spread[slot, PAD:2 * PAD, c], spread[slot, 2 * PAD:3 * PAD, c])
            lanes = pl.ds(pl.multiple_of(g * LANES, LANES), LANES)
            warm[0, :, lanes] = half + half
            warm[1, :, lanes] = final
            fin[g, 0] = energy[0:LEV]
            fin[g, 1] = final[0:LEV]
        return carry
    lax.fori_loop(0, GROUPS // 2, two_groups, 0)

    def gather(i, d):
        for r, g in enumerate(slots_for(d)):
            block = fin[jnp.maximum(g, 0)]
            block = jnp.where(g >= 0, block, 0.0)
            for f in range(2):
                send[i, :, f, r * LANES:(r + 1) * LANES] = block[f]

    def send_final(i, carry):
        gather(i, peer(gy, i, 1))
        state_copy(i).start()
        return carry
    lax.fori_loop(WAVES[2], WAVES[3], send_final, 0)

    mean_sc[...] = jnp.zeros((2 * PAD, LANES), F32)

    def add_end(i, carry):
        lanes = pl.ds(pl.multiple_of(i * 512, 512), 512)
        hi, lo = split(jnp.concatenate([warm[0, :, lanes], warm[1, :, lanes]], axis=0), 2)
        e = spread_of[:, lanes]
        mean_sc[...] += dot(hi, e, NT) + dot(lo, e, NT)
        return carry
    lax.fori_loop(0, 8, add_end, 0)
    tendency = mean_sc[...] * (1.0 / CRM_X) - first
    back = hot((row // 8 == col % 32) & (row % 8 == col // 32))
    r1s[...] = pick_rows(back, tendency, NT).reshape(32, 8, LANES)[:, 0:NX]
    for i in range(NY - 1):
        tendency_copy(i).start()
    r1r[gy] = r1s[gy]

    lax.fori_loop(WAVES[3], NY - 1, send_final, 0)
    gather(31, gy)
    own = pltpu.make_async_copy(send.at[31], out_ref.at[:, :, own_lanes], own_sem)
    own.start()

    def take_coef(i, carry):
        coef_copy(i).wait()
        return carry
    lax.fori_loop(0, RAW, take_coef, 0)
    came = split(c6r[...].reshape(RAW * 8, 3 * PAD).T, 2)

    def finish(i, carry):
        raw_copy(i).wait()
        repeat_ends(raw, i)
        e = hot(iota((RAW * 8, 256), 0) == i * 8 + iota((RAW * 8, 256), 1) // CRM_X)
        both = dot(came[0], e, NN) + dot(came[1], e, NN)
        start = peer(gy, i, -1) * 256
        for r in range(2):
            c = both[:, r * LANES:(r + 1) * LANES]
            lanes = pl.ds(pl.multiple_of(start + r * LANES, LANES), LANES)
            energy, final, _ = physics(
                raw, i, slice(r * LANES, (r + 1) * LANES), c[0:PAD], c[PAD:2 * PAD], c[2 * PAD:3 * PAD])
            out_ref[:, 0, lanes] = energy[0:LEV]
            out_ref[:, 1, lanes] = (c[PAD - 1:PAD] * final)[0:LEV]
        return carry
    lax.fori_loop(0, RAW, finish, 0)

    for i in range(NY - 1):
        tendency_copy(i).wait()
    rows = iota((LANES, 256), 0)
    cols = iota((LANES, 256), 1)
    r2s[...] = pick_rows(
        hot((rows % 32 == cols // 8) & (rows // 32 == cols % 8)),
        jnp.concatenate([r1r[...], jnp.zeros((NY, 8 - NX, LANES), F32)], axis=1).reshape(256, LANES))
    stage4 = []
    for i, tx in enumerate(peers_x):
        copy = pltpu.make_async_remote_copy(
            src_ref=r2s.at[pl.ds(pl.multiple_of(tx * 32, 32), 32), :], dst_ref=r2r.at[own_rows, :],
            send_sem=s4.at[i], recv_sem=v4.at[i], device_id={"gx": tx}, device_id_type=MESH,
        )
        copy.start()
        stage4.append(copy)
    r2r[own_rows, :] = r2s[own_rows, :]

    for copy in stage4:
        copy.wait()
    placed = pick(r2r[...].T, chosen, NT)
    tend_ref[:, 0, :] = placed[0:LEV]
    tend_ref[:, 1, :] = placed[PAD:PAD + LEV]

    own.wait()

    def wait_final(i, carry):
        state_copy(i).wait()
        return carry
    lax.fori_loop(RAW, NY - 1, wait_final, 0)


def on_device(gcm_state, crm_state, send_source, group_owner):
    vm = pltpu.VMEM
    dma = pltpu.SemaphoreType.DMA
    hbm = pl.BlockSpec(memory_space=pltpu.HBM)
    vmem = pl.BlockSpec(memory_space=pltpu.VMEM)
    crm_next, tendency = pl.pallas_call(
        step_kernel,
        out_shape=(jax.ShapeDtypeStruct((LEV, 2, 8192), F32), jax.ShapeDtypeStruct((LEV, 2, LANES), F32)),
        in_specs=[hbm] * 4,
        out_specs=(vmem, vmem),
        scratch_shapes=[
            vm((GROUPS, LEV + 2, 2, LANES), F32), vm((3, LEV, LANES), F32), vm((1, LANES), jnp.int32), vm((4, PAD, LANES), F32),
            vm((2, 128, LANES), F32), vm((2, 128, LANES), F32),
            vm((32, 8, LANES), F32), vm((32, 8, LANES), F32),
            vm((32, NX, LANES), F32), vm((32, NX, LANES), F32),
            vm((128, LANES), F32), vm((128, LANES), F32),
            vm((2, 3 * PAD, 256), F32), vm((LANES, 4096), BF16),
            vm((GROUPS, 2, LEV, LANES), F32), vm((2, PAD, 4096), F32),
            vm((32, LEV, 2, 256), F32), vm((2 * PAD, LANES), F32), vm((2, 3 * PAD, LANES), BF16),
            vm((RAW, 8, 3 * PAD), F32), vm((RAW, 8, 3 * PAD), F32), vm((GROUPS, 8, 3 * PAD), F32), vm((RAW, LEV + 2, 2, 256), F32),
            pltpu.SMEM((GROUPS,), jnp.int32), dma((GROUPS,)), dma, dma, dma, dma, dma((3,)), dma((3,)), dma((31,)), dma((31,)), dma((31,)), dma((31,)),
            dma((3,)), dma((3,)), dma((31,)), dma((31,)), dma((RAW,)), dma((RAW,)),
        ],
        compiler_params=pltpu.CompilerParams(collective_id=0, has_side_effects=True, vmem_limit_bytes=48 << 20),
    )(*[pltpu.with_memory_space_constraint(a, pltpu.HBM) for a in (
        group_owner, send_source.reshape(1, LANES), gcm_state, crm_state.transpose(1, 0, 2))])
    return tendency.transpose(1, 0, 2), crm_next.transpose(1, 0, 2)


def solution(mesh):
    spec = P(None, None, ("gx", "gy"))
    flat = P(("gx", "gy"))
    return jax.shard_map(
        on_device, mesh=mesh, in_specs=(spec, spec, flat, flat), out_specs=(spec, spec), check_vma=False)
```

time: 66.7 us -> 63.2 us (0.948)
  Pallas kernels: 63.4 us -> 59.9 us
    pallas_call x1, Pallas kernels: 63.4 us -> 59.9 us  [on_device(): pl.pallas_call(step_kernel, out_shape=(jax.ShapeDtypeStruct((LEV, 2, 8192...]
where the time goes in v3:
time: 63.2 us; the launch traced here: 63 us
  Pallas kernels  59.9 us (95%)
  local copies, waits for them, and re-layouts  2.51 us (4%)
  between operations  0.64 us (1%)
    pallas_call x1, Pallas kernels, on_device(): pl.pallas_call(step_kernel, out_shape=(jax.ShapeDtypeStruct((LEV, 2, 8192...  59.9 us
    unnamed x2, local copies, waits for them, and re-layouts  2.51 us

profile of v3, /device:TPU:1, one launch (start us, length us, event | category | flops | bytes accessed | tf_op | source)
XLA Modules:
  0.0 63.0 jit_solution(2138040797252890218)
XLA Ops:
  0.6 59.9 %shard_map.59 = (f32[58,2,8192]{2,1,0:T(2,128)S(1)}, f32[58,2,128]{2,1,0:T(2,128)S(1)}) custom-call(s32[32]{0:T(128)} %owner_hbm.1, s32[1,128]{1,0:T(1,128)} %bitcast.7, f32[3,58,128]{2,1,0:T(8,128)} %gcm_hbm.1, f32[58,2,4096]{2,1,0:T(2,128)} %bitcast.6), custom_call_target="tpu_custom_call" | custom-call | tf_op jit(solution)/shard_map/pallas_call | solution.py:393
  60.5 0.6 copy.8
  61.1 1.9 %copy.9 = f32[2,58,8192]{2,0,1:T(2,128)} copy(f32[2,58,8192]{2,0,1:T(2,128)S(1)} %bitcast.4) | data formatting | bytes 7602176

commit v4 on v3

--- a/solution.py
+++ b/solution.py
@@ -383,6 +383,33 @@
         state_copy(i).wait()
         return carry
     lax.fori_loop(RAW, NY - 1, wait_final, 0)
+
+
+PARTS = 8
+
+
+def write_kernel(tend_ref, state_ref, tend_out, state_out, tend_sem, sems):
+    tend = pltpu.make_async_copy(tend_ref, tend_out, tend_sem)
+    copies = []
+    for k in range(PARTS):
+        lev = slice(k * 8, min(k * 8 + 8, LEV))
+        copies.append(pltpu.make_async_copy(state_ref.at[lev], state_out.at[lev], sems.at[k]))
+    for copy in copies + [tend]:
+        copy.start()
+    for copy in copies + [tend]:
+        copy.wait()
+
+
+def write_out(tendency, crm_next):
+    vmem = pl.BlockSpec(memory_space=pltpu.VMEM)
+    hbm = pl.BlockSpec(memory_space=pltpu.HBM)
+    return pl.pallas_call(
+        write_kernel,
+        out_shape=(jax.ShapeDtypeStruct((LEV, 2, LANES), F32), jax.ShapeDtypeStruct((LEV, 2, 8192), F32)),
+        in_specs=[vmem, vmem], out_specs=(hbm, hbm),
+        scratch_shapes=[pltpu.SemaphoreType.DMA, pltpu.SemaphoreType.DMA((PARTS,))],
+        compiler_params=pltpu.CompilerParams(vmem_limit_bytes=8 << 20),
+    )(tendency, crm_next)
 
 
 def on_device(gcm_state, crm_state, send_source, group_owner):
@@ -411,6 +438,7 @@
         compiler_params=pltpu.CompilerParams(collective_id=0, has_side_effects=True, vmem_limit_bytes=48 << 20),
     )(*[pltpu.with_memory_space_constraint(a, pltpu.HBM) for a in (
         group_owner, send_source.reshape(1, LANES), gcm_state, crm_state.transpose(1, 0, 2))])
+    tendency, crm_next = write_out(tendency, crm_next)
     return tendency.transpose(1, 0, 2), crm_next.transpose(1, 0, 2)
 
 

time: 63.2 us -> 62.6 us (level)
  local copies, waits for them, and re-layouts: 2.51 us -> 0 us
  Pallas kernels: 59.9 us -> 61.8 us
    unnamed x2 -> x0, local copies, waits for them, and re-layouts: 2.51 us -> none
    pallas_call x0 -> x1, Pallas kernels: none -> 1.95 us  [write_out(): pl.pallas_call(write_kernel, out_shape=(jax.ShapeDtypeStruct((LEV, 2, LAN...]
where the time goes in v4:
time: 62.6 us; the launch traced here: 62.4 us
  Pallas kernels  61.8 us (99%)
  between operations  0.64 us (1%)
    pallas_call x1, Pallas kernels, on_device(): pl.pallas_call(step_kernel, out_shape=(jax.ShapeDtypeStruct((LEV, 2, 8192...  59.9 us
    pallas_call x1, Pallas kernels, write_out(): pl.pallas_call(write_kernel, out_shape=(jax.ShapeDtypeStruct((LEV, 2, LAN...  1.95 us

profile of v4, /device:TPU:1, one launch (start us, length us, event | category | flops | bytes accessed | tf_op | source)
XLA Modules:
  0.0 62.4 jit_solution(1457209046649981442)
XLA Ops:
  0.6 59.9 %shard_map.59 = (f32[58,2,8192]{2,1,0:T(2,128)S(1)}, f32[58,2,128]{2,1,0:T(2,128)S(1)}) custom-call(s32[32]{0:T(128)} %owner_hbm.1, s32[1,128]{1,0:T(1,128)} %bitcast.5, f32[3,58,128]{2,1,0:T(8,128)} %gcm_hbm.1, f32[58,2,4096]{2,1,0:T(2,128)} %bitcast.4), custom_call_target="tpu_custom_call" | custom-call | tf_op jit(solution)/shard_map/pallas_call | solution.py:420
  60.5 2.0 %shard_map.60 = (f32[58,2,128]{2,1,0:T(2,128)}, f32[58,2,8192]{2,1,0:T(2,128)}) custom-call(f32[58,2,128]{2,1,0:T(2,128)S(1)} %get-tuple-element.6.tend_ref, f32[58,2,8192]{2,1,0:T(2,128)S(1)} %get-tuple-element.7.state_ref), custom_call_target="tpu_custom_call" | custom-call | tf_op jit(solution)/shard_map/pallas_call | solution.py:406
